TPU v7x, 256 devices: a whole 4x4x8 slice. The times are simulated.
256 devices in a mesh: plane: 16 (over x, z_lo, core), tm: 16 (over y, z_hi).
Axes of the slice: x: 4, y: 4, z: 8 (z_hi: 4, z_lo: 2; z = z_hi * 2 + z_lo), core: 2. Of those that a mesh axis runs over, the one named last changes fastest.
Arguments:
- coeffs: float32 [64, 3, 16, 2048], P('tm', None, None, 'plane'), may hold values from -1.5 to 1.5
- radius: float32 [2048], P('plane'), may hold values from 0.25 to 2
- tile_mask: int32 [4, 16, 1], P(None, 'plane'), may hold values from 0 to 1
Outputs:
- hazard: float32 [4, 2048], P(None, 'plane')
All inputs are finite; a program needn't handle non-finite values.
Results may differ from a plain program's by a relative error of at most 0.0003.
Values sent between devices are 32-bit elements; how exact they have to be, the bound alone decides.
A program may use at most 64 MiB of HBM per device.

v0:
```python
import jax
import jax.numpy as jnp
from jax import lax
from jax.sharding import Mesh
from jax.sharding import PartitionSpec as P

SAMP = 32
TILE = 128
ROUNDS = 4
TM = ("tm_0", "tm_1")


def one_axis_at_a_time(value, axes):
    for axis in axes:
        value = lax.psum(value, axis)
    return value


def from_behind(value, axis, steps):
    count = lax.axis_size(axis)
    pairs = [(source, (source + steps) % count) for source in range(count)]
    return lax.ppermute(value, axis, pairs)


def basis_table(degrees):
    sample = jnp.arange(SAMP, dtype=jnp.float32)
    nodes = -1.0 + (2.0 * sample + 1.0) / SAMP
    series = [jnp.ones_like(nodes), nodes]
    for degree in range(2, degrees):
        series.append(2.0 * nodes * series[-1] - series[-2])
    return jnp.stack(series[:degrees], axis=1)


def synthesize(basis, coeff_block):
    return jnp.einsum("sk,wckn->wcsn", basis, coeff_block, precision=lax.Precision.HIGHEST)


def tile_values(own_pos, own_rad, far_pos, far_rad):
    inverse = 1.0 / (own_rad[:, None] + far_rad[None, :])
    separation = own_pos[:, :, :, :, None] - far_pos[:, :, :, None, :]
    squared = jnp.sum(separation * separation, axis=1)
    return jnp.sum(jnp.exp(-squared * inverse), axis=(0, 1))


def paired_sums(own_pos, own_rad, far_pos, far_rad, row_mask, column_mask):
    block_size = own_pos.shape[3]
    tile_count = block_size // TILE

    def visit(pair_index, carry):
        own_tile = pair_index // tile_count
        far_tile = pair_index % tile_count
        row_weight = row_mask[own_tile, far_tile]
        column_weight = column_mask[far_tile, own_tile]

        def compute(current):
            rows_now, columns_now = current
            values = tile_values(own_pos, own_rad, far_pos, far_rad)
            row_part = row_weight * jnp.sum(values, axis=1)
            column_part = column_weight * jnp.sum(values, axis=0)
            row_before = rows_now
            column_before = columns_now
            rows_now = row_before + row_part
            columns_now = column_before + column_part
            return (rows_now, columns_now)

        return lax.cond(row_weight + column_weight > 0, compute, lambda unchanged: unchanged, carry)

    empty = jnp.zeros((block_size,), jnp.float32)
    return lax.fori_loop(0, tile_count * tile_count, visit, (empty, empty))


def local(coeffs, radius, tile_mask):
    plane_count = lax.axis_size("plane")
    time_count = lax.axis_size(TM)
    basis = basis_table(coeffs.shape[2])
    own_pos = synthesize(basis, coeffs)
    normalizer = 1.0 / (coeffs.shape[0] * time_count * SAMP * TILE)
    mask_float = tile_mask.astype(jnp.float32)

    def finish(round_sum):
        return one_axis_at_a_time(round_sum, TM) * normalizer

    round_rows = []
    for pair_no in range(ROUNDS // 2):
        offset = pair_no + 1
        arrived, arrived_rad, arrived_mask = from_behind(
            (coeffs, radius, mask_float[2 * pair_no + 1]), "plane", offset % plane_count
        )
        far_pos = synthesize(basis, arrived)
        row_sums, column_sums = paired_sums(
            own_pos, radius, far_pos, arrived_rad, mask_float[2 * pair_no], arrived_mask
        )
        returned = from_behind(column_sums, "plane", -offset % plane_count)
        round_rows.append(finish(row_sums))
        round_rows.append(finish(returned))
    return jnp.stack(round_rows)


def solution(mesh):
    torus = Mesh(mesh.devices.reshape(mesh.shape["plane"], 4, 4), ("plane", "tm_0", "tm_1"))
    in_specs = (P(TM, None, None, "plane"), P("plane"), P(None, "plane", None))
    out_specs = P(None, "plane")
    return jax.shard_map(local, mesh=torus, in_specs=in_specs, out_specs=out_specs, check_vma=False)
```

profile of v0, /device:TPU:38, one launch (start us, length us, event | category | flops | bytes accessed | tf_op | source)
XLA Modules:
  0.0 83.4 jit_solution(16997058259667615335)
XLA Ops:
  0.0 0.0 collective-permute-start.1
  0.0 1.8 %collective-permute-start.5 = (f32[4,3,16,128]{3,2,1,0:T(8,128)}, f32[4,3,16,128]{3,2,1,0:T(8,128)S(1)}, u32[]{:S(2)}, u32[]{:S(2)}) collective-permute-start(f32[4,3,16,128]{3,2,1,0:T(8,128)} %param.7), channel_id=1, source_target_pairs={{0,32},{16,48},{32,64},{48,80},{64,96},{80,112},{96,128},{112,144}... | collective-permute-start | bytes 294920 | tf_op jit(solution)/shard_map/ppermute | solution.py:22
  1.8 0.1 collective-permute-start.2
  1.9 0.9 %collective-permute-start.6 = (f32[128]{0:T(128)}, f32[128]{0:T(128)S(1)}, u32[]{:S(2)}, u32[]{:S(2)}) collective-permute-start(f32[128]{0:T(128)} %param.8), channel_id=1, source_target_pairs={{0,32},{16,48},{32,64},{48,80},{64,96},{80,112},{96,128},{112,144}... | collective-permute-start | bytes 1544 | tf_op jit(solution)/shard_map/ppermute | solution.py:22
  2.8 0.7 convert_element_type.11
  3.5 0.7 fusion.7
  4.1 0.0 collective-permute-start
  4.4 0.1 stack.12
  4.4 1.2 %convolution_bitcast_fusion.2 = f32[4,3,32,128]{3,2,1,0:T(8,128)S(1)} fusion(f32[4,3,16,128]{3,2,1,0:T(8,128)} %param.7, f32[32,16]{0,1:T(8,128)S(1)} %stack.12), kind=kOutput, calls=%fused_computation.16 | convolution fusion | flops 9437184 | bytes 296960 | tf_op jit(solution)/shard_map/sk,wckn->wcsn/dot_general | solution.py:35
  5.7 1.5 %collective-permute-done = f32[1,1]{1,0:T(1,128)} collective-permute-done((f32[1,1]{1,0:T(1,128)}, f32[1,1]{1,0:T(1,128)}, u32[]{:S(2)}, u32[]{:S(2)}) %collective-permute-start) | collective-permute-done | bytes 36 | tf_op jit(solution)/shard_map/ppermute | solution.py:22
  7.2 4.0 %collective-permute-start.4 = (f32[1,1]{1,0:T(1,128)}, f32[1,1]{1,0:T(1,128)}, u32[]{:S(2)}, u32[]{:S(2)}) collective-permute-start(f32[1,1]{1,0:T(1,128)} %bitcast.11), channel_id=1, source_target_pairs={{0,32},{16,48},{32,64},{48,80},{64,96},{80,112},{96,128},{112,144}... | collective-permute-start | bytes 20 | tf_op jit(solution)/shard_map/ppermute | solution.py:22
  12.5 0.2 collective-permute-done.4
  14.0 0.0 collective-permute-done.1
  14.0 0.4 convolution_bitcast_fusion.1
  14.4 0.0 collective-permute-done.2
  14.4 18.6 %conditional.2 = (f32[128]{0:T(128)S(1)}, f32[128]{0:T(128)S(1)}) conditional(s32[]{:T(128)} %convert_element_type.12, f32[128]{0:T(128)S(1)} %broadcast.442, (f32[]{:T(128)}, f32[4,3,32,128]{3,2,1,0:T(8,128)S(1)}, f32[4,3,32,128]{3,2,1,0:T(8,128)S(1)}, f32[128]{0:T(128)}, f32[128]{0:T(128)S(1)}, /*index=5*/f32[128]{0:T(128)S(1)}, f32[]{:T(128)}) %tuple.23), branch_computations={%region_0.1_spmd, %region_1.0_spmd} | conditional | flops 25198848 | bytes 17308212 | solution.py:66
  14.4 0.0 copy-start
  14.5 11.6 %multiply_reduce_fusion = f32[4,32,128,128]{3,2,1,0:T(8,128)} fusion(f32[4,3,32,128]{3,2,1,0:T(8,128)S(1)} %get-tuple-element.70, f32[4,3,32,128]{3,2,1,0:T(8,128)S(1)} %get-tuple-element.69), kind=kLoop, calls=%fused_computation | loop fusion | flops 16777216 | bytes 8781824 | tf_op jit(solution)/shard_map/while/body/eval_jaxpr/cond/branch_1_fun/reduce_sum | solution.py:41
  26.0 0.0 copy-done
  26.1 0.1 add_divide_fusion
  26.1 5.6 %fusion = (f32[128]{0:T(128)S(1)}, f32[128]{0:T(128)S(1)}) fusion(f32[4,32,128,128]{3,2,1,0:T(8,128)} %multiply_reduce_fusion, f32[128,128]{1,0:T(8,128)S(1)} %add_divide_fusion), kind=kLoop, calls=%fused_computation.2 | loop fusion | flops 8388352 | bytes 8455168 | tf_op jit(solution)/shard_map/while/body/eval_jaxpr/cond/branch_1_fun/reduce_sum | solution.py:59
  31.7 1.3 %multiply_add_fusion = (f32[128]{0:T(128)S(1)}, f32[128]{0:T(128)S(1)}) fusion(f32[128]{0:T(128)S(1)} %get-tuple-element.67, f32[128]{0:T(128)S(1)} %get-tuple-element.109, f32[]{:T(128)} %get-tuple-element.75, f32[128]{0:T(128)S(1)} %get-tuple-element.120, f32[]{:T(128)} %get-tuple-element.68), kind=kLoop, calls=%fused_computation.5 | loop fusion | flops 512 | bytes 2568 | tf_op jit(solution)/shard_map/while/body/eval_jaxpr/cond/branch_1_fun/add | solution.py:63
  33.0 0.1 collective-permute-start.3
  33.1 0.0 collective-permute-done.5
  33.1 0.4 convolution_bitcast_fusion
  33.5 0.0 collective-permute-done.6
  33.5 18.8 %conditional.3 = (f32[128]{0:T(128)S(1)}, f32[128]{0:T(128)S(1)}) conditional(s32[]{:T(128)} %convert_element_type.13, f32[128]{0:T(128)S(1)} %broadcast.442, (f32[]{:T(128)}, f32[4,3,32,128]{3,2,1,0:T(8,128)S(1)}, f32[4,3,32,128]{3,2,1,0:T(8,128)S(1)}, f32[128]{0:T(128)}, f32[128]{0:T(128)S(1)}, /*index=5*/f32[128]{0:T(128)S(1)}, f32[]{:T(128)}) %tuple.24), branch_computations={%region_9.10_spmd, %region_10.14_spmd} | conditional | flops 25198848 | bytes 17308212 | solution.py:66
  33.7 0.0 copy-start.1
  33.7 11.6 %multiply_reduce_fusion.1 = f32[4,32,128,128]{3,2,1,0:T(8,128)} fusion(f32[4,3,32,128]{3,2,1,0:T(8,128)S(1)} %get-tuple-element.79, f32[4,3,32,128]{3,2,1,0:T(8,128)S(1)} %get-tuple-element.78), kind=kLoop, calls=%fused_computation.7 | loop fusion | flops 16777216 | bytes 8781824 | tf_op jit(solution)/shard_map/while/body/eval_jaxpr/cond/branch_1_fun/reduce_sum | solution.py:41
  45.3 0.0 copy-done.1
  45.3 0.1 add_divide_fusion.1
  45.4 5.6 %fusion.2 = (f32[128]{0:T(128)S(1)}, f32[128]{0:T(128)S(1)}) fusion(f32[4,32,128,128]{3,2,1,0:T(8,128)} %multiply_reduce_fusion.1, f32[128,128]{1,0:T(8,128)S(1)} %add_divide_fusion.1), kind=kLoop, calls=%fused_computation.9 | loop fusion | flops 8388352 | bytes 8455168 | tf_op jit(solution)/shard_map/while/body/eval_jaxpr/cond/branch_1_fun/reduce_sum | solution.py:59
  51.0 1.3 %multiply_add_fusion.2 = (f32[128]{0:T(128)S(1)}, f32[128]{0:T(128)S(1)}) fusion(f32[128]{0:T(128)S(1)} %get-tuple-element.76, f32[128]{0:T(128)S(1)} %get-tuple-element.122, f32[]{:T(128)} %get-tuple-element.100, f32[128]{0:T(128)S(1)} %get-tuple-element.124, f32[]{:T(128)} %get-tuple-element.77), kind=kLoop, calls=%fused_computation.12 | loop fusion | flops 512 | bytes 2568 | tf_op jit(solution)/shard_map/while/body/eval_jaxpr/cond/branch_1_fun/add | solution.py:63
  52.3 0.1 collective-permute-start.7
  52.4 0.0 collective-permute-done.3
  52.4 5.6 %collective-permute-done.7 = f32[128]{0:T(128)S(1)} collective-permute-done((f32[128]{0:T(128)S(1)}, f32[128]{0:T(128)S(1)}, u32[]{:S(2)}, u32[]{:S(2)}) %collective-permute-start.7) | collective-permute-done | bytes 544 | tf_op jit(solution)/shard_map/ppermute | solution.py:22
  58.0 10.7 %all-reduce.1 = (f32[128]{0:T(128)S(1)}, f32[128]{0:T(128)S(1)}, f32[128]{0:T(128)S(1)}, f32[128]{0:T(128)S(1)}) all-reduce(f32[128]{0:T(128)S(1)} %collective-permute-done.7, f32[128]{0:T(128)S(1)} %get-tuple-element.107, f32[128]{0:T(128)S(1)} %collective-permute-done.3, ...), channel_id=1, replica_groups=mesh['plane'=16,'tm_0'=4,'tm_1'=4] {'tm_0'}, use_global_device_ids=true, to_apply=%region_16.17 | all-reduce | flops 512 | bytes 4096 | tf_op jit(solution)/shard_map/psum | solution.py:15
  68.7 14.0 %all-reduce = (f32[128]{0:T(128)S(1)}, f32[128]{0:T(128)S(1)}, f32[128]{0:T(128)S(1)}, f32[128]{0:T(128)S(1)}) all-reduce(f32[128]{0:T(128)S(1)} %get-tuple-element.129, f32[128]{0:T(128)S(1)} %get-tuple-element.130, f32[128]{0:T(128)S(1)} %get-tuple-element.131, ...), channel_id=1, replica_groups=mesh['plane'=16,'tm_0'=4,'tm_1'=4] {'tm_1'}, use_global_device_ids=true, to_apply=%region_17.18 | all-reduce | flops 512 | bytes 4096 | tf_op jit(solution)/shard_map/psum | solution.py:15
  82.8 0.6 pad_maximum_fusion
  (14 shorter events, 0.2 us)
Async XLA Ops:
  0.0 14.0 %collective-permute-start.1 = (f32[4,3,16,128]{3,2,1,0:T(8,128)}, f32[4,3,16,128]{3,2,1,0:T(8,128)S(1)}, u32[]{:S(2)}, u32[]{:S(2)}) collective-permute-start(f32[4,3,16,128]{3,2,1,0:T(8,128)} %param.7), channel_id=1, source_target_pairs={{0,16},{16,32},{32,48},{48,64},{64,80},{80,96},{96,112},{112,128},... | collective-permute-start | bytes 294920 | tf_op jit(solution)/shard_map/ppermute | solution.py:22
  0.0 33.1 %collective-permute-start.5 = (f32[4,3,16,128]{3,2,1,0:T(8,128)}, f32[4,3,16,128]{3,2,1,0:T(8,128)S(1)}, u32[]{:S(2)}, u32[]{:S(2)}) collective-permute-start(f32[4,3,16,128]{3,2,1,0:T(8,128)} %param.7), channel_id=1, source_target_pairs={{0,32},{16,48},{32,64},{48,80},{64,96},{80,112},{96,128},{112,144}... | collective-permute-start | bytes 294920 | tf_op jit(solution)/shard_map/ppermute | solution.py:22
  1.8 12.6 %collective-permute-start.2 = (f32[128]{0:T(128)}, f32[128]{0:T(128)S(1)}, u32[]{:S(2)}, u32[]{:S(2)}) collective-permute-start(f32[128]{0:T(128)} %param.8), channel_id=1, source_target_pairs={{0,16},{16,32},{32,48},{48,64},{64,80},{80,96},{96,112},{112,128},... | collective-permute-start | bytes 1544 | tf_op jit(solution)/shard_map/ppermute | solution.py:22
  1.9 31.6 %collective-permute-start.6 = (f32[128]{0:T(128)}, f32[128]{0:T(128)S(1)}, u32[]{:S(2)}, u32[]{:S(2)}) collective-permute-start(f32[128]{0:T(128)} %param.8), channel_id=1, source_target_pairs={{0,32},{16,48},{32,64},{48,80},{64,96},{80,112},{96,128},{112,144}... | collective-permute-start | bytes 1544 | tf_op jit(solution)/shard_map/ppermute | solution.py:22
  4.1 3.1 %collective-permute-start = (f32[1,1]{1,0:T(1,128)}, f32[1,1]{1,0:T(1,128)}, u32[]{:S(2)}, u32[]{:S(2)}) collective-permute-start(f32[1,1]{1,0:T(1,128)} %bitcast.1), channel_id=1, source_target_pairs={{0,16},{16,32},{32,48},{48,64},{64,80},{80,96},{96,112},{112,128},... | collective-permute-start | bytes 20 | tf_op jit(solution)/shard_map/ppermute | solution.py:22
  7.2 5.5 %collective-permute-start.4 = (f32[1,1]{1,0:T(1,128)}, f32[1,1]{1,0:T(1,128)}, u32[]{:S(2)}, u32[]{:S(2)}) collective-permute-start(f32[1,1]{1,0:T(1,128)} %bitcast.11), channel_id=1, source_target_pairs={{0,32},{16,48},{32,64},{48,80},{64,96},{80,112},{96,128},{112,144}... | collective-permute-start | bytes 20 | tf_op jit(solution)/shard_map/ppermute | solution.py:22
  14.4 11.6 %copy-start = (f32[128]{0:T(128)S(1)}, f32[128]{0:T(128)}, u32[]{:S(2)}) copy-start(f32[128]{0:T(128)} %get-tuple-element.71) | copy-start | bytes 1540 | tf_op jit(solution)/shard_map/while/body/eval_jaxpr/cond
  33.0 19.4 %collective-permute-start.3 = (f32[128]{0:T(128)S(1)}, f32[128]{0:T(128)S(1)}, u32[]{:S(2)}, u32[]{:S(2)}) collective-permute-start(f32[128]{0:T(128)S(1)} %get-tuple-element.106), channel_id=1, source_target_pairs={{0,240},{16,0},{32,16},{48,32},{64,48},{80,64},{96,80},{112,96},{1... | collective-permute-start | bytes 1544 | tf_op jit(solution)/shard_map/ppermute | solution.py:22
  33.7 11.6 %copy-start.1 = (f32[128]{0:T(128)S(1)}, f32[128]{0:T(128)}, u32[]{:S(2)}) copy-start(f32[128]{0:T(128)} %get-tuple-element.80) | copy-start | bytes 1540 | tf_op jit(solution)/shard_map/while/body/eval_jaxpr/cond
  52.3 5.7 %collective-permute-start.7 = (f32[128]{0:T(128)S(1)}, f32[128]{0:T(128)S(1)}, u32[]{:S(2)}, u32[]{:S(2)}) collective-permute-start(f32[128]{0:T(128)S(1)} %get-tuple-element.108), channel_id=1, source_target_pairs={{0,224},{16,240},{32,0},{48,16},{64,32},{80,48},{96,64},{112,80},{... | collective-permute-start | bytes 1544 | tf_op jit(solution)/shard_map/ppermute | solution.py:22
where the time goes:
time: 83.7 us; the launch traced here: 83.4 us
  other arithmetic  38.6 us (46%)
  blocking collectives  24.7 us (30%)
  waiting for transfers between devices  7.31 us (9%)
  starting transfers between devices  7.04 us (8%)
  between operations  2.74 us (3%)
  matrix products  1.96 us (2%)
    psum x2, blocking collectives, one_axis_at_a_time(): value = lax.psum(value, axis)  24.7 us
    reduce_sum x2, other arithmetic, tile_values(): squared = jnp.sum(separation * separation, axis=1)  23.2 us
    reduce_sum x2, other arithmetic, compute(): column_part = column_weight * jnp.sum(values, axis=0)  11.1 us
    ppermute x8, waiting for transfers between devices, from_behind(): return lax.ppermute(value, axis, pairs)  7.31 us
    ppermute x8, starting transfers between devices, from_behind(): return lax.ppermute(value, axis, pairs)  7.04 us
    add x2, other arithmetic, compute(): columns_now = column_before + column_part  2.62 us
    dot_general x3, matrix products, synthesize(): jnp.einsum('sk,wckn->wcsn', basis, coeff_block, precision=lax.Precision.H...  1.96 us
  transfers between devices with their start and end apart: 8, of which 3 were waited for; matrix products, arithmetic and copies ran while one was open for 49% of the time, Pallas kernels for 0%

commit v1 on v0

v1 whole, which is shorter than its diff:
```python
import functools

import jax
import jax.numpy as jnp
from jax import lax
from jax.experimental import pallas as pl
from jax.experimental.pallas import tpu as pltpu
from jax.sharding import Mesh
from jax.sharding import PartitionSpec as P

SAMP = 32
TILE = 128
ROUNDS = 4
K = 16
WIN = 4
FEATS = 24
SUB = 8
LOG2E = 1.4426950408889634
TM = ("tm_0", "tm_1")
MESH = pl.DeviceIdType.MESH
f32 = jnp.float32
bf16 = jnp.bfloat16


def split3(x):
    h = x.astype(bf16).astype(f32)
    rest = x - h
    m = rest.astype(bf16).astype(f32)
    return h, m, rest - m


def basis_parts():
    shape = (SAMP, 5 * K)
    sample = lax.broadcasted_iota(jnp.int32, shape, 0).astype(f32)
    lane = lax.broadcasted_iota(jnp.int32, shape, 1)
    degree = lane % K
    t = -1.0 + (2.0 * sample + 1.0) / SAMP
    before, now = jnp.ones_like(t), t
    table = jnp.where(degree == 0, before, now)
    for k in range(2, K):
        before, now = now, 2.0 * t * now - before
        table = jnp.where(degree == k, now, table)
    h, m, l = split3(table)
    part = lane // K
    return jnp.where(part == 4, l, jnp.where(part == 2, m, h)).astype(bf16)


def positions(basis, coef):
    n = coef.shape[1]
    h, m, l = split3(coef)
    columns = []
    for c in range(3):
        rows = slice(K * c, K * c + K)
        columns.append(jnp.concatenate([h[rows], m[rows], h[rows], l[rows], h[rows]], axis=0).astype(bf16))
    pos = jnp.dot(basis, jnp.concatenate(columns, axis=1), preferred_element_type=f32)
    return [pos[:, c * n : (c + 1) * n] for c in range(3)]


def features(pos, own):
    parts = [split3(p) for p in pos]
    norm = pos[0] * pos[0] + pos[1] * pos[1] + pos[2] * pos[2]
    norms = list(split3(norm))
    ones = [jnp.ones_like(norm)] * 3
    if own:
        return [-2.0 * parts[c][r] for r in (0, 0, 1, 0, 2, 1) for c in range(3)] + ones + norms
    return [parts[c][r] for r in (0, 1, 0, 2, 0, 1) for c in range(3)] + norms + ones


def stacked(feats, b):
    return jnp.concatenate([f[SUB * b : SUB * b + SUB] for f in feats], axis=0)


def kernel(
    coef, rad, mask, out,
    own, own_rad, own_mask, far, far_rad, lhs, mean, scale, acc, part_r, part_c, mine, step1, step1_c, step2,
    load_sem, send_sem, recv_sem, rad_send, rad_recv, r_send, r_recv, c_send, c_recv, y_send, y_recv,
):
    planes = lax.axis_size("plane")
    g = lax.axis_index("plane")
    y = lax.axis_index("tm_0")
    z = lax.axis_index("tm_1")

    def plane(step):
        return lax.rem(g + step + planes, planes)

    def other(i, step):
        return lax.rem(i + step, 4)

    barrier = pltpu.get_barrier_semaphore()

    def greet(device):
        pl.semaphore_signal(barrier, inc=1, device_id=device, device_id_type=MESH)

    for d in (1, 2):
        greet((plane(-d), y, z))
        for k in range(4):
            greet((plane(d), y, other(z, k)))
    for k in (1, 2, 3):
        greet((g, y, other(z, k)))
        greet((g, other(y, k), z))

    loads = [
        pltpu.make_async_copy(coef, own, load_sem.at[0]),
        pltpu.make_async_copy(rad, own_rad, load_sem.at[1]),
        pltpu.make_async_copy(mask, own_mask, load_sem.at[2]),
    ]
    for copy in loads:
        copy.start()
    basis = basis_parts()

    pl.semaphore_wait(barrier, 16)

    def coef_copy(w, d):
        return pltpu.make_async_remote_copy(
            src_ref=coef.at[w], dst_ref=far.at[d, w], send_sem=send_sem.at[d, w], recv_sem=recv_sem.at[d, w],
            device_id=(plane(d + 1), y, z), device_id_type=MESH,
        )

    def rad_copy(d):
        return pltpu.make_async_remote_copy(
            src_ref=rad, dst_ref=far_rad.at[d], send_sem=rad_send.at[d], recv_sem=rad_recv.at[d],
            device_id=(plane(d + 1), y, z), device_id_type=MESH,
        )

    for d in range(2):
        rad_copy(d).start()
    for w in range(WIN):
        for d in range(2):
            coef_copy(w, d).start()

    for copy in loads:
        copy.wait()

    def prepare(w, carry):
        c = own[w]
        mu = jnp.mean(c, axis=1, keepdims=True)
        mean[w] = jnp.broadcast_to(mu, c.shape)
        feats = features(positions(basis, c - mu), True)
        for b in range(SAMP // SUB):
            lhs[w, b] = stacked(feats, b).T.astype(bf16)
        return carry

    lax.fori_loop(0, WIN, prepare, 0)

    for d in range(2):
        rad_copy(d).wait_recv()
    column = jnp.broadcast_to(own_rad[...], (TILE, TILE)).T
    for d in range(2):
        scale[:, TILE * d : TILE * d + TILE] = -LOG2E / (column + far_rad[d])
    acc[...] = jnp.zeros_like(acc)

    rows = 32
    turn = lax.broadcasted_iota(jnp.int32, (rows, FEATS * SUB), 1) % SUB

    def window(w, carry):
        for d in range(2):
            coef_copy(w, d).wait_recv()
        mu = mean[w]
        c = jnp.concatenate([far[0, w] - mu, far[1, w] - mu], axis=1)
        feats = features(positions(basis, c), False)
        for b in range(SAMP // SUB):
            rhs = stacked(feats, b).astype(bf16)
            for i in range(TILE // rows):
                here = slice(rows * i, rows * i + rows)
                left = lhs[w, b, here, :]
                zero = jnp.zeros_like(left)
                big = jnp.concatenate([jnp.where(turn == s, left, zero) for s in range(SUB)], axis=0)
                dist = jnp.dot(big, rhs, preferred_element_type=f32)
                sc = scale[here, :]
                total = None
                for s in range(SUB):
                    term = jnp.exp2(dist[rows * s : rows * s + rows] * sc)
                    total = term if total is None else total + term
                acc[here, :] += total
        return carry

    lax.fori_loop(0, WIN, window, 0)

    sums = acc[...]
    part_r[0:1, :] = jnp.sum(sums[:, :TILE].T, axis=0, keepdims=True)
    part_r[1:2, :] = jnp.sum(sums[:, TILE:].T, axis=0, keepdims=True)
    column_sums = jnp.sum(sums, axis=0, keepdims=True)
    for d in range(2):
        part_c[d] = column_sums[:, TILE * d : TILE * d + TILE]

    def row_copy(k, slot):
        return pltpu.make_async_remote_copy(
            src_ref=part_r, dst_ref=step1.at[slot], send_sem=r_send.at[k], recv_sem=r_recv.at[slot],
            device_id=(g, y, other(z, k)), device_id_type=MESH,
        )

    def column_copy(d, k, slot):
        return pltpu.make_async_remote_copy(
            src_ref=part_c.at[d], dst_ref=step1_c.at[d, slot], send_sem=c_send.at[d, k], recv_sem=c_recv.at[d, slot],
            device_id=(plane(-d - 1), y, other(z, k)), device_id_type=MESH,
        )

    for k in range(4):
        for d in range(2):
            column_copy(d, k, z).start()
        if k:
            row_copy(k, z).start()
    step1[z] = part_r[...]
    for k in range(4):
        if k:
            row_copy(k, other(z, k)).wait_recv()
        for d in range(2):
            column_copy(d, k, other(z, k)).wait_recv()
    mine[0:2, :] = (step1[0] + step1[1]) + (step1[2] + step1[3])
    for d in range(2):
        mine[2 + d : 3 + d, :] = (step1_c[d, 0] + step1_c[d, 1]) + (step1_c[d, 2] + step1_c[d, 3])

    def y_copy(k, slot):
        return pltpu.make_async_remote_copy(
            src_ref=mine, dst_ref=step2.at[slot], send_sem=y_send.at[k], recv_sem=y_recv.at[slot],
            device_id=(g, other(y, k), z), device_id_type=MESH,
        )

    for k in (1, 2, 3):
        y_copy(k, y).start()
    step2[y] = mine[...]
    for k in (1, 2, 3):
        y_copy(k, other(y, k)).wait_recv()
    total = (step2[0] + step2[1]) + (step2[2] + step2[3])
    for d in range(2):
        for row, r in ((d, 2 * d), (2 + d, 2 * d + 1)):
            line = total[row : row + 1, :]
            out[r : r + 1, :] = jnp.where(own_mask[0, r] > 0, line, jnp.zeros_like(line))

    for d in range(2):
        rad_copy(d).wait_send()
        for w in range(WIN):
            coef_copy(w, d).wait_send()
    for k in range(4):
        for d in range(2):
            column_copy(d, k, z).wait_send()
        if k:
            row_copy(k, z).wait_send()
            y_copy(k, y).wait_send()


def local(coeffs, radius, tile_mask):
    vmem = pltpu.VMEM
    dma = pltpu.SemaphoreType.DMA
    sums = pl.pallas_call(
        kernel,
        out_shape=jax.ShapeDtypeStruct((4, TILE), f32),
        in_specs=[pl.BlockSpec(memory_space=pltpu.HBM)] * 3,
        out_specs=pl.BlockSpec(memory_space=pltpu.VMEM),
        scratch_shapes=[
            vmem((WIN, 3 * K, TILE), f32),
            vmem((1, TILE), f32),
            pltpu.SMEM((1, ROUNDS), jnp.int32),
            vmem((2, WIN, 3 * K, TILE), f32),
            vmem((2, 1, TILE), f32),
            vmem((WIN, SAMP // SUB, TILE, FEATS * SUB), bf16),
            vmem((WIN, 3 * K, TILE), f32),
            vmem((TILE, 2 * TILE), f32),
            vmem((TILE, 2 * TILE), f32),
            vmem((2, TILE), f32),
            vmem((2, 1, TILE), f32),
            vmem((4, TILE), f32),
            vmem((4, 2, TILE), f32),
            vmem((2, 4, 1, TILE), f32),
            vmem((4, 4, TILE), f32),
            dma((3,)),
            dma((2, WIN)),
            dma((2, WIN)),
            dma((2,)),
            dma((2,)),
            dma((4,)),
            dma((4,)),
            dma((2, 4)),
            dma((2, 4)),
            dma((4,)),
            dma((4,)),
        ],
        compiler_params=pltpu.CompilerParams(
            collective_id=0, has_side_effects=True, vmem_limit_bytes=32 << 20
        ),
    )(*[pltpu.with_memory_space_constraint(x, pltpu.HBM) for x in (coeffs.reshape(WIN, 3 * K, TILE), radius.reshape(1, TILE), tile_mask.reshape(1, ROUNDS))])
    time_count = lax.axis_size(TM)
    normalizer = 1.0 / (coeffs.shape[0] * time_count * SAMP * TILE)
    return sums * normalizer


def solution(mesh):
    torus = Mesh(mesh.devices.reshape(mesh.shape["plane"], 4, 4), ("plane", "tm_0", "tm_1"))
    in_specs = (P(TM, None, None, "plane"), P("plane"), P(None, "plane", None))
    out_specs = P(None, "plane")
    return jax.shard_map(local, mesh=torus, in_specs=in_specs, out_specs=out_specs, check_vma=False)
```

time: 83.7 us -> 25.4 us (0.30)
  the two profiles are of different devices: /device:TPU:38 before, /device:TPU:1 now
where the time goes in v1:
time: 25.4 us; the launch traced here: 25.3 us
  Pallas kernels  24.7 us (97%)
  other arithmetic  0.58 us (2%)
    pallas_call x1, Pallas kernels, local(): pl.pallas_call(kernel, out_shape=jax.ShapeDtypeStruct((4, TILE), f32), in...  24.7 us
    mul x1, other arithmetic, local(): return sums * normalizer  0.58 us

profile of v1, /device:TPU:1, one launch (start us, length us, event | category | flops | bytes accessed | tf_op | source)
XLA Modules:
  0.0 25.3 jit_solution(3880505531997518042)
XLA Ops:
  0.0 24.7 %shard_map.37 = f32[4,128]{1,0:T(4,128)S(1)} custom-call(f32[4,48,128]{2,1,0:T(8,128)} %bitcast.3, f32[1,128]{1,0:T(1,128)} %bitcast.4, s32[1,4]{1,0:T(1,128)} %bitcast.5), custom_call_target="tpu_custom_call" | custom-call | tf_op jit(solution)/shard_map/pallas_call | solution.py:245
  24.7 0.6 %broadcast_multiply_fusion = f32[4,128]{1,0:T(4,128)} fusion(f32[4,128]{1,0:T(4,128)S(1)} %shard_map.37), kind=kLoop, calls=%fused_computation | loop fusion | flops 512 | bytes 4096 | tf_op jit(solution)/shard_map/mul | solution.py:284

commit v2 on v1

--- a/solution.py
+++ b/solution.py
@@ -1,5 +1,3 @@
-import functools
-
 import jax
 import jax.numpy as jnp
 from jax import lax
@@ -17,6 +15,9 @@
 SUB = 8
 LOG2E = 1.4426950408889634
 TM = ("tm_0", "tm_1")
+FAR_FIRST = sorted(
+    ((a, k) for a in range(4) for k in range(4)), key=lambda s: -(min(s[0], 4 - s[0]) + 2 * min(s[1], 4 - s[1]))
+)
 MESH = pl.DeviceIdType.MESH
 f32 = jnp.float32
 bf16 = jnp.bfloat16
@@ -72,8 +73,8 @@
 
 def kernel(
     coef, rad, mask, out,
-    own, own_rad, own_mask, far, far_rad, lhs, mean, scale, acc, part_r, part_c, mine, step1, step1_c, step2,
-    load_sem, send_sem, recv_sem, rad_send, rad_recv, r_send, r_recv, c_send, c_recv, y_send, y_recv,
+    own, own_rad, own_mask, far, far_rad, lhs, mean, scale, acc, part_r, part_c, all_r, all_c,
+    load_sem, send_sem, recv_sem, rad_send, rad_recv, r_send, r_recv, c_send, c_recv, known_z, known_plane,
 ):
     planes = lax.axis_size("plane")
     g = lax.axis_index("plane")
@@ -93,9 +94,7 @@
 
     for d in (1, 2):
         greet((plane(-d), y, z))
-        for k in range(4):
-            greet((plane(d), y, other(z, k)))
-    for k in (1, 2, 3):
+    for k in (2, 1, 3):
         greet((g, y, other(z, k)))
         greet((g, other(y, k), z))
 
@@ -108,7 +107,9 @@
         copy.start()
     basis = basis_parts()
 
-    pl.semaphore_wait(barrier, 16)
+    pl.semaphore_wait(barrier, 8)
+    for k in (2, 1, 3):
+        pl.semaphore_signal(known_z, inc=1, device_id=(g, y, other(z, k)), device_id_type=MESH)
 
     def coef_copy(w, d):
         return pltpu.make_async_remote_copy(
@@ -174,7 +175,11 @@
                 acc[here, :] += total
         return carry
 
-    lax.fori_loop(0, WIN, window, 0)
+    lax.fori_loop(0, WIN // 2, window, 0)
+    pl.semaphore_wait(known_z, 3)
+    for d in (1, 2):
+        pl.semaphore_signal(known_plane, inc=1, device_id=(plane(d), y, z), device_id_type=MESH)
+    lax.fori_loop(WIN // 2, WIN, window, 0)
 
     sums = acc[...]
     part_r[0:1, :] = jnp.sum(sums[:, :TILE].T, axis=0, keepdims=True)
@@ -183,60 +188,47 @@
     for d in range(2):
         part_c[d] = column_sums[:, TILE * d : TILE * d + TILE]
 
-    def row_copy(k, slot):
-        return pltpu.make_async_remote_copy(
-            src_ref=part_r, dst_ref=step1.at[slot], send_sem=r_send.at[k], recv_sem=r_recv.at[slot],
-            device_id=(g, y, other(z, k)), device_id_type=MESH,
-        )
-
-    def column_copy(d, k, slot):
-        return pltpu.make_async_remote_copy(
-            src_ref=part_c.at[d], dst_ref=step1_c.at[d, slot], send_sem=c_send.at[d, k], recv_sem=c_recv.at[d, slot],
-            device_id=(plane(-d - 1), y, other(z, k)), device_id_type=MESH,
-        )
-
-    for k in range(4):
-        for d in range(2):
-            column_copy(d, k, z).start()
-        if k:
-            row_copy(k, z).start()
-    step1[z] = part_r[...]
-    for k in range(4):
-        if k:
-            row_copy(k, other(z, k)).wait_recv()
-        for d in range(2):
-            column_copy(d, k, other(z, k)).wait_recv()
-    mine[0:2, :] = (step1[0] + step1[1]) + (step1[2] + step1[3])
-    for d in range(2):
-        mine[2 + d : 3 + d, :] = (step1_c[d, 0] + step1_c[d, 1]) + (step1_c[d, 2] + step1_c[d, 3])
-
-    def y_copy(k, slot):
-        return pltpu.make_async_remote_copy(
-            src_ref=mine, dst_ref=step2.at[slot], send_sem=y_send.at[k], recv_sem=y_recv.at[slot],
-            device_id=(g, other(y, k), z), device_id_type=MESH,
-        )
-
-    for k in (1, 2, 3):
-        y_copy(k, y).start()
-    step2[y] = mine[...]
-    for k in (1, 2, 3):
-        y_copy(k, other(y, k)).wait_recv()
-    total = (step2[0] + step2[1]) + (step2[2] + step2[3])
-    for d in range(2):
-        for row, r in ((d, 2 * d), (2 + d, 2 * d + 1)):
-            line = total[row : row + 1, :]
-            out[r : r + 1, :] = jnp.where(own_mask[0, r] > 0, line, jnp.zeros_like(line))
+    def row_copy(a, k, ys, zs):
+        slot = 4 * ys + zs
+        return pltpu.make_async_remote_copy(
+            src_ref=part_r, dst_ref=all_r.at[slot], send_sem=r_send.at[a, k], recv_sem=r_recv.at[slot],
+            device_id=(g, other(y, a), other(z, k)), device_id_type=MESH,
+        )
+
+    def column_copy(d, a, k, ys, zs):
+        slot = 4 * ys + zs
+        return pltpu.make_async_remote_copy(
+            src_ref=part_c.at[d], dst_ref=all_c.at[d, slot], send_sem=c_send.at[d, a, k], recv_sem=c_recv.at[d, slot],
+            device_id=(plane(-d - 1), other(y, a), other(z, k)), device_id_type=MESH,
+        )
+
+    pl.semaphore_wait(known_plane, 2)
+    for a, k in FAR_FIRST:
+        for d in range(2):
+            column_copy(d, a, k, y, z).start()
+        if a or k:
+            row_copy(a, k, y, z).start()
+    all_r[4 * y + z] = part_r[...]
 
     for d in range(2):
         rad_copy(d).wait_send()
         for w in range(WIN):
             coef_copy(w, d).wait_send()
-    for k in range(4):
-        for d in range(2):
-            column_copy(d, k, z).wait_send()
-        if k:
-            row_copy(k, z).wait_send()
-            y_copy(k, y).wait_send()
+    for a, k in reversed(FAR_FIRST):
+        for d in range(2):
+            column_copy(d, a, k, y, z).wait_send()
+        if a or k:
+            row_copy(a, k, y, z).wait_send()
+
+    for a, k in reversed(FAR_FIRST):
+        if a or k:
+            row_copy(a, k, other(y, a), other(z, k)).wait_recv()
+        for d in range(2):
+            column_copy(d, a, k, other(y, a), other(z, k)).wait_recv()
+    rows_total = jnp.sum(all_r[...], axis=0)
+    for d in range(2):
+        for r, line in ((2 * d, rows_total[d : d + 1, :]), (2 * d + 1, jnp.sum(all_c[d], axis=0))):
+            out[r : r + 1, :] = jnp.where(own_mask[0, r] > 0, line, jnp.zeros_like(line))
 
 
 def local(coeffs, radius, tile_mask):
@@ -259,21 +251,19 @@
             vmem((TILE, 2 * TILE), f32),
             vmem((2, TILE), f32),
             vmem((2, 1, TILE), f32),
-            vmem((4, TILE), f32),
-            vmem((4, 2, TILE), f32),
-            vmem((2, 4, 1, TILE), f32),
-            vmem((4, 4, TILE), f32),
+            vmem((16, 2, TILE), f32),
+            vmem((2, 16, 1, TILE), f32),
             dma((3,)),
             dma((2, WIN)),
             dma((2, WIN)),
             dma((2,)),
             dma((2,)),
-            dma((4,)),
-            dma((4,)),
-            dma((2, 4)),
-            dma((2, 4)),
-            dma((4,)),
-            dma((4,)),
+            dma((4, 4)),
+            dma((16,)),
+            dma((2, 4, 4)),
+            dma((2, 16)),
+            pltpu.SemaphoreType.REGULAR,
+            pltpu.SemaphoreType.REGULAR,
         ],
         compiler_params=pltpu.CompilerParams(
             collective_id=0, has_side_effects=True, vmem_limit_bytes=32 << 20

time: 25.4 us -> 24.3 us (0.957)
  Pallas kernels: 24.7 us -> 23.6 us
    pallas_call x1, Pallas kernels: 24.7 us -> 23.6 us  [local(): pl.pallas_call(kernel, out_shape=jax.ShapeDtypeStruct((4, TILE), f32), in...]
where the time goes in v2:
time: 24.3 us; the launch traced here: 24.2 us
  Pallas kernels  23.6 us (97%)
  other arithmetic  0.58 us (2%)
    pallas_call x1, Pallas kernels, local(): pl.pallas_call(kernel, out_shape=jax.ShapeDtypeStruct((4, TILE), f32), in...  23.6 us
    mul x1, other arithmetic, local(): return sums * normalizer  0.58 us

profile of v2, /device:TPU:1, one launch (start us, length us, event | category | flops | bytes accessed | tf_op | source)
XLA Modules:
  0.0 24.2 jit_solution(5435625702232777191)
XLA Ops:
  0.0 23.6 %shard_map.37 = f32[4,128]{1,0:T(4,128)S(1)} custom-call(f32[4,48,128]{2,1,0:T(8,128)} %bitcast.3, f32[1,128]{1,0:T(1,128)} %bitcast.4, s32[1,4]{1,0:T(1,128)} %bitcast.5), custom_call_target="tpu_custom_call" | custom-call | tf_op jit(solution)/shard_map/pallas_call | solution.py:237
  23.7 0.6 %broadcast_multiply_fusion = f32[4,128]{1,0:T(4,128)} fusion(f32[4,128]{1,0:T(4,128)S(1)} %shard_map.37), kind=kLoop, calls=%fused_computation | loop fusion | flops 512 | bytes 4096 | tf_op jit(solution)/shard_map/mul | solution.py:274

commit v3 on v2

--- a/solution.py
+++ b/solution.py
@@ -74,7 +74,7 @@
 def kernel(
     coef, rad, mask, out,
     own, own_rad, own_mask, far, far_rad, lhs, mean, scale, acc, part_r, part_c, all_r, all_c,
-    load_sem, send_sem, recv_sem, rad_send, rad_recv, r_send, r_recv, c_send, c_recv, known_z, known_plane,
+    load_sem, send_sem, recv_sem, rad_send, rad_recv, r_send, r_recv, c_send, c_recv, known,
 ):
     planes = lax.axis_size("plane")
     g = lax.axis_index("plane")
@@ -94,8 +94,9 @@
 
     for d in (1, 2):
         greet((plane(-d), y, z))
+    for k in (1, 3):
+        greet((g, y, other(z, k)))
     for k in (2, 1, 3):
-        greet((g, y, other(z, k)))
         greet((g, other(y, k), z))
 
     loads = [
@@ -107,9 +108,15 @@
         copy.start()
     basis = basis_parts()
 
-    pl.semaphore_wait(barrier, 8)
-    for k in (2, 1, 3):
-        pl.semaphore_signal(known_z, inc=1, device_id=(g, y, other(z, k)), device_id_type=MESH)
+    pl.semaphore_wait(barrier, 7)
+
+    def tell(turn, devices):
+        for device in devices:
+            pl.semaphore_signal(known.at[turn], inc=1, device_id=device, device_id_type=MESH)
+
+    next_z = [(g, y, other(z, k)) for k in (1, 3)]
+    next_plane = [(plane(d), y, z) for d in (1, 2)]
+    tell(0, next_z)
 
     def coef_copy(w, d):
         return pltpu.make_async_remote_copy(
@@ -142,6 +149,8 @@
         return carry
 
     lax.fori_loop(0, WIN, prepare, 0)
+    pl.semaphore_wait(known.at[0], 2)
+    tell(1, next_z)
 
     for d in range(2):
         rad_copy(d).wait_recv()
@@ -173,13 +182,15 @@
                     term = jnp.exp2(dist[rows * s : rows * s + rows] * sc)
                     total = term if total is None else total + term
                 acc[here, :] += total
+
+        @pl.when(w == 0)
+        def _():
+            pl.semaphore_wait(known.at[1], 2)
+            tell(2, next_plane)
+
         return carry
 
-    lax.fori_loop(0, WIN // 2, window, 0)
-    pl.semaphore_wait(known_z, 3)
-    for d in (1, 2):
-        pl.semaphore_signal(known_plane, inc=1, device_id=(plane(d), y, z), device_id_type=MESH)
-    lax.fori_loop(WIN // 2, WIN, window, 0)
+    lax.fori_loop(0, WIN, window, 0)
 
     sums = acc[...]
     part_r[0:1, :] = jnp.sum(sums[:, :TILE].T, axis=0, keepdims=True)
@@ -202,7 +213,7 @@
             device_id=(plane(-d - 1), other(y, a), other(z, k)), device_id_type=MESH,
         )
 
-    pl.semaphore_wait(known_plane, 2)
+    pl.semaphore_wait(known.at[2], 2)
     for a, k in FAR_FIRST:
         for d in range(2):
             column_copy(d, a, k, y, z).start()
@@ -262,8 +273,7 @@
             dma((16,)),
             dma((2, 4, 4)),
             dma((2, 16)),
-            pltpu.SemaphoreType.REGULAR,
-            pltpu.SemaphoreType.REGULAR,
+            pltpu.SemaphoreType.REGULAR((3,)),
         ],
         compiler_params=pltpu.CompilerParams(
             collective_id=0, has_side_effects=True, vmem_limit_bytes=32 << 20

time: 24.3 us -> 23 us (0.947)
  Pallas kernels: 23.6 us -> 22.1 us
    pallas_call x1, Pallas kernels: 23.6 us -> 22.1 us  [local(): pl.pallas_call(kernel, out_shape=jax.ShapeDtypeStruct((4, TILE), f32), in...]
where the time goes in v3:
time: 23 us; the launch traced here: 22.7 us
  Pallas kernels  22.1 us (96%)
  other arithmetic  0.58 us (3%)
    pallas_call x1, Pallas kernels, local(): pl.pallas_call(kernel, out_shape=jax.ShapeDtypeStruct((4, TILE), f32), in...  22.1 us
    mul x1, other arithmetic, local(): return sums * normalizer  0.58 us

profile of v3, /device:TPU:1, one launch (start us, length us, event | category | flops | bytes accessed | tf_op | source)
XLA Modules:
  0.0 22.7 jit_solution(1931223905767499491)
XLA Ops:
  0.0 22.1 %shard_map.37 = f32[4,128]{1,0:T(4,128)S(1)} custom-call(f32[4,48,128]{2,1,0:T(8,128)} %bitcast.3, f32[1,128]{1,0:T(1,128)} %bitcast.4, s32[1,4]{1,0:T(1,128)} %bitcast.5), custom_call_target="tpu_custom_call" | custom-call | tf_op jit(solution)/shard_map/pallas_call | solution.py:248
  22.1 0.6 %broadcast_multiply_fusion = f32[4,128]{1,0:T(4,128)} fusion(f32[4,128]{1,0:T(4,128)S(1)} %shard_map.37), kind=kLoop, calls=%fused_computation | loop fusion | flops 512 | bytes 4096 | tf_op jit(solution)/shard_map/mul | solution.py:284

commit v4 on v3

--- a/solution.py
+++ b/solution.py
@@ -120,24 +120,24 @@
 
     def coef_copy(w, d):
         return pltpu.make_async_remote_copy(
-            src_ref=coef.at[w], dst_ref=far.at[d, w], send_sem=send_sem.at[d, w], recv_sem=recv_sem.at[d, w],
+            src_ref=own.at[w], dst_ref=far.at[d, w], send_sem=send_sem.at[d, w], recv_sem=recv_sem.at[d, w],
             device_id=(plane(d + 1), y, z), device_id_type=MESH,
         )
 
     def rad_copy(d):
         return pltpu.make_async_remote_copy(
-            src_ref=rad, dst_ref=far_rad.at[d], send_sem=rad_send.at[d], recv_sem=rad_recv.at[d],
+            src_ref=own_rad, dst_ref=far_rad.at[d], send_sem=rad_send.at[d], recv_sem=rad_recv.at[d],
             device_id=(plane(d + 1), y, z), device_id_type=MESH,
         )
+
+    for copy in loads:
+        copy.wait()
 
     for d in range(2):
         rad_copy(d).start()
     for w in range(WIN):
         for d in range(2):
             coef_copy(w, d).start()
-
-    for copy in loads:
-        copy.wait()
 
     def prepare(w, carry):
         c = own[w]

time: 23 us -> 22.8 us (level)
  no operation moved by 1% of the time
where the time goes in v4:
time: 22.8 us; the launch traced here: 22.5 us
  Pallas kernels  21.9 us (96%)
  other arithmetic  0.58 us (3%)
    pallas_call x1, Pallas kernels, local(): pl.pallas_call(kernel, out_shape=jax.ShapeDtypeStruct((4, TILE), f32), in...  21.9 us
    mul x1, other arithmetic, local(): return sums * normalizer  0.58 us

profile of v4, /device:TPU:1, one launch (start us, length us, event | category | flops | bytes accessed | tf_op | source)
XLA Modules:
  0.0 22.5 jit_solution(7705551454444681128)
XLA Ops:
  0.0 21.9 %shard_map.37 = f32[4,128]{1,0:T(4,128)S(1)} custom-call(f32[4,48,128]{2,1,0:T(8,128)} %bitcast.3, f32[1,128]{1,0:T(1,128)} %bitcast.4, s32[1,4]{1,0:T(1,128)} %bitcast.5), custom_call_target="tpu_custom_call" | custom-call | tf_op jit(solution)/shard_map/pallas_call | solution.py:248
  22.0 0.6 %broadcast_multiply_fusion = f32[4,128]{1,0:T(4,128)} fusion(f32[4,128]{1,0:T(4,128)S(1)} %shard_map.37), kind=kLoop, calls=%fused_computation | loop fusion | flops 512 | bytes 4096 | tf_op jit(solution)/shard_map/mul | solution.py:284
